TPU v7x, 1024 devices: a whole 8x8x8 slice. The times are simulated.
1024 devices in a mesh: hidden: 16 (over y_lo, z), width: 8 (over x), replica: 8 (over y_hi, core).
Axes of the slice: x: 8, y: 8 (y_hi: 4, y_lo: 2; y = y_hi * 2 + y_lo), z: 8, core: 2. Of those that a mesh axis runs over, the one named last changes fastest.
Arguments:
- saved_input: bfloat16 [2048, 12288], P(('replica', 'hidden'), 'width'), may hold values from -0.75 to 0.75
- grad_out: bfloat16 [2048, 24576], P(('replica', 'width'), 'hidden'), may hold values from -16 to 16
- weight: bfloat16 [12288, 24576], P('width', 'hidden'), may hold values from -0.0546875 to 0.0546875
- samples: int32 [64], replicated, may hold values from 8 to 16
- correct: int32 [64], replicated, may hold values from 0 to 8
- prompt_ids: int32 [2048], P('replica'), may hold values from 0 to 63
Outputs:
- grad_input: bfloat16 [2048, 12288], P(('replica', 'hidden'), 'width')
- grad_weight: float32 [12288, 24576], P(('width', 'replica'), 'hidden')
Inputs may be any that keep to these rules, and one draw needn't show every extreme that they name: correct[i] <= samples[i] for every prompt.
All inputs are finite; a program needn't handle non-finite values.
Results may differ from a plain program's by a relative error of at most 0.012.
Values may be sent and summed in bfloat16 or wider, within the bound.
A program may use at most 64 MiB of HBM per device.

v0:
```python
import jax
import jax.numpy as jnp
from jax import lax
from jax.sharding import PartitionSpec as P

K = 4


def pass_weights(samples, correct):
    total = samples.astype(jnp.float32)
    good = correct.astype(jnp.float32)
    missing = jnp.ones_like(total)
    for factor_index in range(K):
        missing = missing * jnp.maximum(total - good - factor_index, 0.0) / (total - factor_index)
    return 1.0 - missing


def token_weights(prompt_ids, samples, correct):
    pass_at_k = pass_weights(samples, correct)
    prompt_range = jnp.arange(samples.shape[0], dtype=jnp.int32)
    matches = prompt_ids[:, None] == prompt_range[None, :]
    picked = jnp.sum(jnp.where(matches, pass_at_k[None, :], 0.0), axis=1)
    rounded = lax.optimization_barrier(picked.astype(jnp.bfloat16))
    return rounded.astype(jnp.float32)


def body(saved_input, grad_out, weight, samples, correct, prompt_ids):
    weights_all = token_weights(prompt_ids, samples, correct)
    gathered_x = lax.all_gather(saved_input, "hidden", axis=0, tiled=True)
    gathered_g = lax.all_gather(grad_out, "width", axis=0, tiled=True)
    scaled = (gathered_g.astype(jnp.float32) * weights_all[:, None]).astype(jnp.bfloat16)
    picked = scaled
    grad_input = lax.psum_scatter(
        lax.dot_general(
            picked, weight, (((1,), (1,)), ((), ())), preferred_element_type=jnp.float32
        ),
        "hidden",
        scatter_dimension=0,
        tiled=True,
    )
    picked = gathered_x
    grad_weight = lax.psum_scatter(
        lax.dot_general(
            picked, scaled, (((0,), (0,)), ((), ())), preferred_element_type=jnp.float32
        ).astype(jnp.bfloat16),
        "replica",
        scatter_dimension=0,
        tiled=True,
    ).astype(jnp.float32)
    return (grad_input.astype(jnp.bfloat16), grad_weight)


def solution(mesh):
    in_specs = (
        P(("replica", "hidden"), "width"),
        P(("replica", "width"), "hidden"),
        P("width", "hidden"),
        P(),
        P(),
        P("replica"),
    )
    out_specs = (P(("replica", "hidden"), "width"), P(("width", "replica"), "hidden"))
    return jax.shard_map(body, mesh=mesh, in_specs=in_specs, out_specs=out_specs, check_vma=False)
```

profile of v0, /device:TPU:1, one launch (start us, length us, event | category | flops | bytes accessed | tf_op | source)
XLA Modules:
  0.0 210.4 jit_solution(10563604368168316530)
XLA Ops:
  7.2 0.0 reduce-scatter.5.cloned.1.call-start
  7.2 0.7 fusion.2
  7.9 0.8 select_reduce_fusion
  8.7 22.1 %all_gather.6 = bf16[256,1536]{1,0:T(8,128)(2,1)S(1)} all-gather(bf16[32,1536]{1,0:T(8,128)(2,1)} %param.7), channel_id=1, replica_groups=mesh['hidden'=16,'width'=8,'replica'=8] {'width'}, dimensions={0}, use_global_device_ids=true | all-gather | bytes 884736 | tf_op jit(solution)/shard_map/all_gather | solution.py:30
  30.8 5.0 %fusion.1 = f32[256,1536]{1,0:T(8,128)} fusion(bf16[1536,1536]{1,0:T(8,128)(2,1)} %param.8, bf16[256,1536]{1,0:T(8,128)(2,1)S(1)} %all_gather.6, f32[256]{0:T(256)S(1)} %convert_element_type.34), kind=kOutput, calls=%fused_computation.3 | convolution fusion | flops 1209139200 | bytes 7078912 | tf_op jit(solution)/shard_map/dot_general | solution.py:34
  35.7 0.0 copy-start
  35.7 0.0 reduce-scatter.5.cloned.1.call-update
  35.7 0.0 reduce-scatter.7.cloned.1.call-start
  35.8 0.7 copy-done
  36.5 44.6 %all_gather.7 = bf16[256,1536]{1,0:T(8,128)(2,1)S(1)} all-gather(bf16[16,1536]{1,0:T(8,128)(2,1)S(1)} %copy-done), channel_id=1, replica_groups=mesh['hidden'=16,'width'=8,'replica'=8] {'hidden'}, dimensions={0}, use_global_device_ids=true | all-gather | bytes 835584 | tf_op jit(solution)/shard_map/all_gather | solution.py:29
  81.1 3.7 %fusion = bf16[1536,1536]{0,1:T(8,128)(2,1)} fusion(bf16[256,1536]{1,0:T(8,128)(2,1)S(1)} %all_gather.7, bf16[256,1536]{1,0:T(8,128)(2,1)S(1)} %all_gather.6, f32[256]{0:T(256)S(1)} %convert_element_type.34), kind=kOutput, calls=%fused_computation.1 | convolution fusion | flops 1211498496 | bytes 6292480 | tf_op jit(solution)/shard_map/dot_general | solution.py:43
  84.8 6.6 %copy.11 = bf16[1536,1536]{1,0:T(8,128)(2,1)} copy(bf16[1536,1536]{0,1:T(8,128)(2,1)} %fusion) | data formatting | bytes 9437184
  91.4 0.0 reduce-scatter.7.cloned.1.call-update
  91.4 31.3 %reduce-scatter.5.cloned.1.call-done = f32[16,1536]{1,0:T(8,128)} async-done(((f32[256,1536]{1,0:T(8,128)}), f32[16,1536]{1,0:T(8,128)}) %reduce-scatter.5.cloned.1.call-update) | async-done | bytes 98320 | tf_op jit(solution)/shard_map/reduce_scatter | solution.py:33
  122.7 1.5 convert_element_type.36
  124.2 76.7 %reduce-scatter.7.cloned.1.call-done = bf16[192,1536]{1,0:T(8,128)(2,1)} async-done(((bf16[1536,1536]{1,0:T(8,128)(2,1)}), bf16[192,1536]{1,0:T(8,128)(2,1)}) %reduce-scatter.7.cloned.1.call-update) | async-done | bytes 589840
  200.9 1.3 copy.12
  202.3 1.3 copy.10
  (1 shorter events, 0.0 us)
Async XLA Ops:
  7.2 115.5 %reduce-scatter.5.cloned.1.call-start = ((), (), s32[]{:S(2)}) async-start(), calls=%async_computation.2 | async-start | bytes 1671168 | tf_op jit(solution)/shard_map/reduce_scatter | solution.py:33
  35.7 0.8 copy-start
  35.7 165.2 %reduce-scatter.7.cloned.1.call-start = ((), (), s32[]{:S(2)}) async-start(), calls=%async_computation.3 | async-start | bytes 5308416
Sparse Core Ops, SparseCore 0:
  35.9 86.8 reduce-scatter.4
  126.1 74.7 reduce-scatter.6
where the time goes:
time: 211 us; the launch traced here: 210 us
  waiting for transfers between devices  108 us (51%)
  blocking collectives  66.6 us (32%)
  between operations  14 us (7%)
  local copies, waits for them, and re-layouts  9.96 us (5%)
  matrix products  8.65 us (4%)
  other arithmetic  2.98 us (1%)
    unnamed x3, waiting for transfers between devices  76.7 us
    all_gather x1, blocking collectives, body(): gathered_x = lax.all_gather(saved_input, 'hidden', axis=0, tiled=True)  44.6 us
    reduce_scatter x1, waiting for transfers between devices, body(): lax.psum_scatter(lax.dot_general(picked, weight, (((1,), (1,)), ((), ()))...  31.3 us
    all_gather x1, blocking collectives, body(): gathered_g = lax.all_gather(grad_out, 'width', axis=0, tiled=True)  22.1 us
    unnamed x5, local copies, waits for them, and re-layouts  9.96 us
    dot_general x1, matrix products, body(): lax.dot_general(picked, weight, (((1,), (1,)), ((), ())), preferred_eleme...  4.97 us
  transfers between devices with their start and end apart: 2, of which 2 were waited for; matrix products, arithmetic and copies ran while one was open for 6% of the time, Pallas kernels for 0%

commit v1 on v0

v1 whole, which is shorter than its diff:
```python
import functools

import jax
import jax.numpy as jnp
from jax import lax
from jax.experimental import pallas as pl
from jax.experimental.pallas import tpu as pltpu
from jax.sharding import PartitionSpec as P

K = 4
MESH = pl.DeviceIdType.MESH
F32 = jnp.float32
BF16 = jnp.bfloat16

NX = 8
NZ = 8
NK = 4
HALF = NX // 2


def pass_weights(samples, correct):
    total = samples.astype(jnp.float32)
    good = correct.astype(jnp.float32)
    missing = jnp.ones_like(total)
    for factor_index in range(K):
        missing = missing * jnp.maximum(total - good - factor_index, 0.0) / (total - factor_index)
    return 1.0 - missing


def token_weights(prompt_ids, samples, correct):
    pass_at_k = pass_weights(samples, correct)
    prompt_range = jnp.arange(samples.shape[0], dtype=jnp.int32)
    matches = prompt_ids[:, None] == prompt_range[None, :]
    picked = jnp.sum(jnp.where(matches, pass_at_k[None, :], 0.0), axis=1)
    rounded = lax.optimization_barrier(picked.astype(jnp.bfloat16))
    return rounded.astype(jnp.float32)


def kernel(
    g_in, x_in, w_hbm, gw_out, gi_out,
    gbuf, xbuf, wv, part, rb1, sb, rb2, acc, xt,
    loc_sem, ring_s, ring_r, cc_s, cc_r, ye_s, ye_r, xa_s, xa_r,
    yl_s, yl_r, zr_s, zr_r, xc_s, xc_r, t1_s, t1_r, t2_s, t2_r,
):
    h = lax.axis_index("hidden")
    w = lax.axis_index("width")
    r = lax.axis_index("replica")
    k, c = r // 2, lax.rem(r, 2)
    yl, z = h // NZ, lax.rem(h, NZ)
    zq, zh = z // 2, lax.rem(z, 2)

    def xdev(d):
        return {"width": lax.rem(w + d + NX, NX)}

    def zdev(d):
        return {"hidden": yl * NZ + lax.rem(z + d + NZ, NZ)}

    def kdev(d):
        return {"replica": lax.rem(k + d, NK) * 2 + c}

    partner = {"replica": k * 2 + 1 - c}
    yldev = {"hidden": (1 - yl) * NZ + z}
    sends = []

    def send(src, dst, ss, rs, dev):
        cp = pltpu.make_async_remote_copy(
            src_ref=src, dst_ref=dst, send_sem=ss, recv_sem=rs, device_id=dev, device_id_type=MESH
        )
        cp.start()
        sends.append(cp)

    def arrived(dst, ss, rs, dev):
        pltpu.make_async_remote_copy(
            src_ref=dst, dst_ref=dst, send_sem=ss, recv_sem=rs, device_id=dev, device_id_type=MESH
        ).wait_recv()

    shift = (0, 1, 3, 2)
    kp = [lax.rem(k + s, NK) for s in shift]

    loads = [
        pltpu.make_async_copy(g_in, gbuf.at[k, w, c], loc_sem.at[0]),
        pltpu.make_async_copy(
            x_in.at[:, pl.ds(pl.multiple_of(k * 384, 384), 384)], xbuf.at[k, yl, zq, c, zh], loc_sem.at[1]
        ),
        pltpu.make_async_copy(w_hbm, wv, loc_sem.at[2]),
    ]
    for cp in loads:
        cp.start()

    bar = pltpu.get_barrier_semaphore()
    for dev in (xdev(1), xdev(-1), zdev(1), zdev(-1), kdev(1), kdev(3), yldev, partner):
        pl.semaphore_signal(bar, inc=1, device_id=dev, device_id_type=MESH)
    pl.semaphore_wait(bar, 8)

    def xa_send(d):
        to = lax.rem(k + d, NK)
        send(
            x_in.at[:, pl.ds(pl.multiple_of(to * 384, 384), 384)],
            xbuf.at[k, yl, zq, c, zh], xa_s.at[d - 1], xa_r.at[d - 1], kdev(d),
        )

    def xa_wait(d):
        frm = lax.rem(k + NK - d, NK)
        arrived(xbuf.at[frm, yl, zq, c, zh], xa_s.at[d - 1], xa_r.at[d - 1], kdev(d))

    def ye_send(d):
        send(g_in, gbuf.at[k, w, c], ye_s.at[d - 1], ye_r.at[d - 1], kdev(d))

    def ye_wait(d):
        frm = lax.rem(k + NK - d, NK)
        arrived(gbuf.at[frm, w, c], ye_s.at[d - 1], ye_r.at[d - 1], kdev(d))

    def blk(p, e, s):
        m = lax.rem(w - e * s + NX, NX)
        ref = gbuf.at[kp[p], m, c]
        return ref.at[0 if e == 1 else 1] if s == HALF else ref

    def fwd_view(p, e, s):
        m = lax.rem(w - e * s + NX, NX)
        ref = gbuf.at[kp[p], m, c]
        return ref.at[0 if e == 1 else 1] if s == HALF - 1 else ref

    def cc_send(p, i, ref, src=None):
        send(ref if src is None else src, ref, cc_s.at[p, i], cc_r.at[p, i], partner)

    def ring_start(p):
        own = gbuf.at[kp[p], w, c]
        src = g_in if p == 0 else own
        for i, e in enumerate((1, -1)):
            send(src, own, ring_s.at[p, i, 0], ring_r.at[p, i, 0], xdev(e))
        cc_send(p, 0, own, src)

    def ring_adv(p, s):
        for i, e in enumerate((1, -1)):
            arrived(blk(p, e, s), ring_s.at[p, i, s - 1], ring_r.at[p, i, s - 1], xdev(e))
            if s < HALF:
                ref = fwd_view(p, e, s)
                send(ref, ref, ring_s.at[p, i, s], ring_r.at[p, i, s], xdev(e))
            cc_send(p, 1 + 2 * (s - 1) + i, blk(p, e, s))

    def cc_wait(p):
        o = 1 - c
        arrived(gbuf.at[kp[p], w, o], cc_s.at[p, 0], cc_r.at[p, 0], partner)
        for s in range(1, HALF + 1):
            for i, e in enumerate((1, -1)):
                m = lax.rem(w - e * s + NX, NX)
                ref = gbuf.at[kp[p], m, o]
                if s == HALF:
                    ref = ref.at[i]
                n = 1 + 2 * (s - 1) + i
                arrived(ref, cc_s.at[p, n], cc_r.at[p, n], partner)

    def zblk(d, last, i):
        zz = lax.rem(z + d + NZ, NZ)
        if last:
            return xbuf.at[:, i, zz // 2, c, lax.rem(zz, 2)]
        return xbuf.at[:, :, zz // 2, c, lax.rem(zz, 2)]

    def z_start():
        for i, e in enumerate((1, -1)):
            ref = zblk(0, False, i)
            send(ref, ref, zr_s.at[i, 0], zr_r.at[i, 0], zdev(e))

    def z_adv(s):
        for i, e in enumerate((1, -1)):
            arrived(zblk(-e * s, s == HALF, i), zr_s.at[i, s - 1], zr_r.at[i, s - 1], zdev(e))
            if s < HALF:
                ref = zblk(-e * s, s == HALF - 1, i)
                send(ref, ref, zr_s.at[i, s], zr_r.at[i, s], zdev(e))

    def t3_dot(n):
        lhs = gbuf[k, :, c].reshape(256, 1536)
        out = lax.dot_general(
            lhs, wv[pl.ds(n * 512, 512), :], (((1,), (1,)), ((), ())), preferred_element_type=F32
        )
        part[:, :, :, pl.ds(n * 512, 512)] = out.astype(BF16).reshape(2, NZ, 16, 512)

    order = (4, 3, 5, 2, 6, 1, 7, 0)

    def t3_send():
        for d in order:
            zz = lax.rem(z + d, NZ)
            send(part.at[1 - yl, zz], rb1.at[d], t1_s.at[d], t1_r.at[d], yldev)

    def t3_pair(d):
        zz = lax.rem(z + d, NZ)
        arrived(rb1.at[d], t1_s.at[d], t1_r.at[d], yldev)
        both = part[yl, zz].astype(F32) + rb1[d].astype(F32)
        sb[d] = both.astype(BF16)

    def t3_out(d):
        if d:
            send(sb.at[d], rb2.at[d], t2_s.at[d], t2_r.at[d], zdev(d))

    def t3_final():
        total = sb[0].astype(F32)
        for d in range(1, NZ):
            arrived(rb2.at[d], t2_s.at[d], t2_r.at[d], zdev(d))
            total = total + rb2[d].astype(F32)
        gi_out[...] = total.astype(BF16)

    win = pl.ds(pl.multiple_of(c * 128, 128), 256)
    owin = pl.ds(pl.multiple_of((1 - c) * 128, 128), 256)

    def xc_send():
        ref = xbuf.at[:, :, :, c, :, :, owin]
        send(ref, ref, xc_s, xc_r, partner)

    def xc_wait():
        ref = xbuf.at[:, :, :, 1 - c, :, :, win]
        arrived(ref, xc_s, xc_r, partner)

    def t4(p):
        xt[...] = xbuf[kp[p], :, :, :, :, :, win].reshape(512, 256).T

        def step(n, _):
            col = pl.ds(pl.multiple_of(n * 512, 512), 512)
            rhs = gbuf[kp[p], :, :, :, :, col].reshape(512, 512)
            out = jnp.dot(xt[...], rhs, preferred_element_type=F32)
            if p == 0:
                acc[:, col] = out
            else:
                acc[:, col] += out
            return 0

        lax.fori_loop(0, 3, step, 0)

    xa_send(1)
    xa_send(3)
    ring_start(0)
    ye_send(1)
    ye_send(3)
    loads[0].wait()
    loads[1].wait()
    xa_wait(1)
    xa_wait(3)
    xa_send(2)
    ye_send(2)
    ring_adv(0, 1)
    ye_wait(3)
    ring_start(1)
    ring_adv(0, 2)
    xa_wait(2)
    ref = xbuf.at[:, yl, zq, c, zh]
    send(ref, ref, yl_s, yl_r, yldev)
    ring_adv(1, 1)
    arrived(xbuf.at[:, 1 - yl, zq, c, zh], yl_s, yl_r, yldev)
    z_start()
    ring_adv(0, 3)
    ring_adv(1, 2)
    ye_wait(1)
    ring_start(2)
    z_adv(1)
    loads[2].wait()
    ring_adv(0, 4)
    t3_dot(0)
    ring_adv(1, 3)
    ring_adv(2, 1)
    t3_dot(1)
    ye_wait(2)
    ring_start(3)
    z_adv(2)
    ring_adv(1, 4)
    t3_dot(2)
    ring_adv(2, 2)
    t3_send()
    ring_adv(3, 1)
    z_adv(3)
    ring_adv(2, 3)
    z_adv(4)
    xc_send()
    late = None
    for n, d in enumerate(order):
        t3_pair(d)
        if late is not None:
            t3_out(late)
        late = d
        if n == 3:
            ring_adv(3, 2)
    ring_adv(2, 4)
    ring_adv(3, 3)
    xc_wait()
    for p in range(3):
        cc_wait(p)
        t4(p)
    t3_final()
    ring_adv(3, 4)
    cc_wait(3)
    t4(3)
    gw_out[...] = acc[pl.ds(pl.multiple_of(c * 64, 64), 192), :]
    for cp in sends:
        cp.wait_send()


def body(saved_input, grad_out, weight, samples, correct, prompt_ids):
    w = lax.axis_index("width")
    own_ids = lax.dynamic_slice(prompt_ids, (w * 32,), (32,))
    weights_own = token_weights(own_ids, samples, correct)
    scaled = (grad_out.astype(F32) * weights_own[:, None]).astype(BF16).reshape(2, 16, 1536)
    dma = pltpu.SemaphoreType.DMA
    vm = pl.BlockSpec(memory_space=pltpu.VMEM)
    gw, gi = pl.pallas_call(
        kernel,
        out_shape=(
            jax.ShapeDtypeStruct((192, 1536), F32),
            jax.ShapeDtypeStruct((16, 1536), BF16),
        ),
        in_specs=[vm, vm, pl.BlockSpec(memory_space=pl.ANY)],
        out_specs=(vm, vm),
        scratch_shapes=[
            pltpu.VMEM((NK, NX, 2, 2, 16, 1536), BF16),
            pltpu.VMEM((NK, 2, 4, 2, 2, 16, 384), BF16),
            pltpu.VMEM((1536, 1536), BF16),
            pltpu.VMEM((2, NZ, 16, 1536), BF16),
            pltpu.VMEM((NZ, 16, 1536), BF16),
            pltpu.VMEM((NZ, 16, 1536), BF16),
            pltpu.VMEM((NZ, 16, 1536), BF16),
            pltpu.VMEM((256, 1536), F32),
            pltpu.VMEM((256, 512), BF16),
            dma((3,)),
            dma((4, 2, HALF)), dma((4, 2, HALF)),
            dma((4, 1 + 2 * HALF)), dma((4, 1 + 2 * HALF)),
            dma((3,)), dma((3,)),
            dma((3,)), dma((3,)),
            dma, dma,
            dma((2, HALF)), dma((2, HALF)),
            dma, dma,
            dma((NZ,)), dma((NZ,)),
            dma((NZ,)), dma((NZ,)),
        ],
        compiler_params=pltpu.CompilerParams(
            collective_id=0, has_side_effects=True, vmem_limit_bytes=56 * 1024 * 1024
        ),
        cost_estimate=pl.CostEstimate(flops=3_000_000_000, bytes_accessed=8_000_000, transcendentals=0),
    )(scaled, saved_input, weight)
    return gi, gw


def solution(mesh):
    in_specs = (
        P(("replica", "hidden"), "width"),
        P(("replica", "width"), "hidden"),
        P("width", "hidden"),
        P(),
        P(),
        P("replica"),
    )
    out_specs = (P(("replica", "hidden"), "width"), P(("width", "replica"), "hidden"))
    return jax.shard_map(body, mesh=mesh, in_specs=in_specs, out_specs=out_specs, check_vma=False)
```

time: 211 us -> 79.4 us (0.38)
  waiting for transfers between devices: 108 us -> 0 us
  Pallas kernels: 0 us -> 71.4 us
  blocking collectives: 66.6 us -> 0 us
  between operations: 14 us -> 0.65 us
  matrix products: 8.65 us -> 0 us
  local copies, waits for them, and re-layouts: 9.96 us -> 4.54 us
    unnamed x3 -> x0, waiting for transfers between devices: 76.7 us -> none
    pallas_call x0 -> x1, Pallas kernels: none -> 71.4 us  [body(): pl.pallas_call(kernel, out_shape=(jax.ShapeDtypeStruct((192, 1536), F32),...]
    all_gather x2 -> x0, blocking collectives: 66.6 us -> none  [the longest x1 44.6 us: body(): gathered_x = lax.all_gather(saved_input, 'hidden', axis=0, tiled=True)]
    reduce_scatter x1 -> x0, waiting for transfers between devices: 31.3 us -> none  [body(): lax.psum_scatter(lax.dot_general(picked, weight, (((1,), (1,)), ((), ()))...]
    dot_general x2 -> x0, matrix products: 8.65 us -> none  [the longest x1 4.97 us: body(): lax.dot_general(picked, weight, (((1,), (1,)), ((), ())), preferred_eleme...]
    unnamed x5 -> x2, local copies, waits for them, and re-layouts: 9.96 us -> 3.78 us
  transfers between devices with their start and end apart: 2 -> 0, of which waited for: 2 -> 0; matrix products, arithmetic and copies ran while one was open for 6% -> 0% of each run, Pallas kernels for 0% -> 0%
where the time goes in v1:
time: 79.4 us; the launch traced here: 79.1 us
  Pallas kernels  71.4 us (90%)
  local copies, waits for them, and re-layouts  4.54 us (6%)
  other arithmetic  2.49 us (3%)
    pallas_call x1, Pallas kernels, body(): pl.pallas_call(kernel, out_shape=(jax.ShapeDtypeStruct((192, 1536), F32),...  71.4 us
    unnamed x2, local copies, waits for them, and re-layouts  3.78 us
    convert_element_type x1, other arithmetic, body(): (grad_out.astype(F32) * weights_own[:, None]).astype(BF16)  1.62 us

profile of v1, /device:TPU:1, one launch (start us, length us, event | category | flops | bytes accessed | tf_op | source)
XLA Modules:
  0.0 79.1 jit_solution(9595850104370495208)
XLA Ops:
  0.6 0.8 dynamic_slice.3
  1.4 0.7 fusion
  2.1 0.2 select_reduce_fusion
  2.3 1.6 %multiply_convert_fusion = bf16[32,1536]{1,0:T(8,128)(2,1)} fusion(bf16[32,1536]{1,0:T(8,128)(2,1)} %param.7, f32[32]{0:T(128)S(1)} %convert_element_type.22), kind=kLoop, calls=%fused_computation | loop fusion | flops 147456 | bytes 196736 | tf_op jit(solution)/shard_map/convert_element_type | solution.py:299
  3.9 71.4 %shard_map.77 = (f32[192,1536]{1,0:T(8,128)}, bf16[16,1536]{1,0:T(8,128)(2,1)}) custom-call(bf16[2,16,1536]{2,1,0:T(8,128)(2,1)} %bitcast.1, bf16[16,1536]{1,0:T(8,128)(2,1)} %x_in.1, bf16[1536,1536]{1,0:T(8,128)(2,1)} %w_hbm.1), custom_call_target="tpu_custom_call" | custom-call | flops 3000000000 | bytes 8000000 | tf_op jit(solution)/shard_map/pallas_call | solution.py:302
  75.3 1.4 %copy.10 = bf16[16,1536]{1,0:T(8,128)(2,1)} copy(bf16[16,1536]{1,0:T(8,128)(2,1)} %get-tuple-element.8) | data formatting | bytes 98304
  76.7 2.4 %copy.11 = f32[192,1536]{1,0:T(8,128)} copy(f32[192,1536]{1,0:T(8,128)} %get-tuple-element.9) | data formatting | bytes 2359296
  (1 shorter events, 0.0 us)

commit v2 on v1

v2 whole, which is shorter than its diff:
```python
import jax
import jax.numpy as jnp
from jax import lax
from jax.experimental import pallas as pl
from jax.experimental.pallas import tpu as pltpu
from jax.sharding import PartitionSpec as P

K = 4
MESH = pl.DeviceIdType.MESH
F32 = jnp.float32
BF16 = jnp.bfloat16

NX = 8
NZ = 8
NK = 4
HALF = NX // 2


def kernel(
    g_in, x_in, w_hbm, smp, cor, ids, gw_out, gi_out,
    g_own, gbuf, xbuf, wv, part, rb1, sb, rb2, acc, xt,
    loc_sem, ring_s, ring_r, co_s, co_r, cc_s, cc_r, ye_s, ye_r, xa_s, xa_r,
    yl_s, yl_r, zr_s, zr_r, xc_s, xc_r, t1_s, t1_r, t2_s, t2_r, in_sem,
):
    h = lax.axis_index("hidden")
    w = lax.axis_index("width")
    r = lax.axis_index("replica")
    k, c = r // 2, lax.rem(r, 2)
    yl, z = h // NZ, lax.rem(h, NZ)
    zq, zh = z // 2, lax.rem(z, 2)

    def xdev(d):
        return {"width": lax.rem(w + d + NX, NX)}

    def zdev(d):
        return {"hidden": yl * NZ + lax.rem(z + d, NZ)}

    def kdev(d):
        return {"replica": lax.rem(k + d, NK) * 2 + c}

    partner = {"replica": k * 2 + 1 - c}
    yldev = {"hidden": (1 - yl) * NZ + z}
    sends = []

    def send(src, dst, ss, rs, dev):
        cp = pltpu.make_async_remote_copy(
            src_ref=src, dst_ref=dst, send_sem=ss, recv_sem=rs, device_id=dev, device_id_type=MESH
        )
        cp.start()
        sends.append(cp)

    def arrived(dst, ss, rs, dev):
        pltpu.make_async_remote_copy(
            src_ref=dst, dst_ref=dst, send_sem=ss, recv_sem=rs, device_id=dev, device_id_type=MESH
        ).wait_recv()

    shift = (0, 1, 3, 2)
    kp = [lax.rem(k + s, NK) for s in shift]

    bar = pltpu.get_barrier_semaphore()
    for dev in (xdev(1), xdev(-1), kdev(1), kdev(3), yldev, partner):
        pl.semaphore_signal(bar, inc=1, device_id=dev, device_id_type=MESH)
    for d in range(1, NZ):

        @pl.when(z + d < NZ)
        def _():
            pl.semaphore_signal(bar, inc=1, device_id=zdev(d), device_id_type=MESH)

    loads = [
        pltpu.make_async_copy(
            x_in.at[:, pl.ds(pl.multiple_of(k * 384, 384), 384)], xbuf.at[k, yl, zq, c, zh], loc_sem.at[1]
        ),
        pltpu.make_async_copy(w_hbm, wv, loc_sem.at[2]),
    ]
    for cp in loads:
        cp.start()

    total = smp[...].astype(F32)
    good = cor[...].astype(F32)
    missing = jnp.ones_like(total)
    for j in range(K):
        missing = missing * jnp.maximum(total - good - j, 0.0) / (total - j)
    pass_at_k = 1.0 - missing
    prompts = lax.broadcasted_iota(jnp.int32, (64, 64), 0) == lax.broadcasted_iota(jnp.int32, (64, 64), 1)
    column = jnp.sum(jnp.where(prompts, jnp.broadcast_to(pass_at_k, (64, 64)), 0.0), axis=1, keepdims=True)
    match = lax.broadcasted_iota(jnp.int32, (64, 256), 0) == jnp.broadcast_to(ids[...], (64, 256))
    picked = jnp.sum(jnp.where(match, jnp.broadcast_to(column, (64, 256)), 0.0), axis=0, keepdims=True)
    rows = lax.broadcasted_iota(jnp.int32, (32, 256), 0) + w * 32
    mine = rows == lax.broadcasted_iota(jnp.int32, (32, 256), 1)
    weight = jnp.sum(jnp.where(mine, jnp.broadcast_to(picked, (32, 256)), 0.0), axis=1, keepdims=True)
    weight = weight.astype(BF16).astype(F32)
    g_own[...] = (g_in[...].astype(F32) * weight).astype(BF16).reshape(2, 16, 1536)

    pl.semaphore_wait(bar, 6 + z)
    for d in range(1, NZ):

        @pl.when(z + d >= NZ)
        def _():
            pl.semaphore_signal(in_sem, inc=1, device_id=zdev(d), device_id_type=MESH)

    def xa_send(d):
        to = lax.rem(k + d, NK)
        send(
            x_in.at[:, pl.ds(pl.multiple_of(to * 384, 384), 384)],
            xbuf.at[k, yl, zq, c, zh], xa_s.at[d - 1], xa_r.at[d - 1], kdev(d),
        )

    def xa_wait(d):
        frm = lax.rem(k + NK - d, NK)
        arrived(xbuf.at[frm, yl, zq, c, zh], xa_s.at[d - 1], xa_r.at[d - 1], kdev(d))

    def ye_send(d):
        send(g_own, gbuf.at[k, w, c], ye_s.at[d - 1], ye_r.at[d - 1], kdev(d))

    def ye_wait(d):
        frm = lax.rem(k + NK - d, NK)
        arrived(gbuf.at[frm, w, c], ye_s.at[d - 1], ye_r.at[d - 1], kdev(d))

    def blk(p, e, s, j, cc):
        m = lax.rem(w - e * s + NX, NX)
        return gbuf.at[kp[p], m, cc, j]

    def halves(i, s):
        return (0, 1) if s < HALF else (i,)

    def ring_start(p):
        own = gbuf.at[kp[p], w, c]
        for j in (0, 1):
            for i, e in enumerate((1, -1)):
                src = g_own.at[j] if p == 0 else own.at[j]
                send(src, own.at[j], ring_s.at[p, i, 0, j], ring_r.at[p, i, 0, j], xdev(e))
        send(g_own if p == 0 else own, own, co_s.at[p], co_r.at[p], partner)

    def ring_adv(p, s):
        for j in (0, 1):
            for i, e in enumerate((1, -1)):
                if j not in halves(i, s):
                    continue
                ref = blk(p, e, s, j, c)
                arrived(ref, ring_s.at[p, i, s - 1, j], ring_r.at[p, i, s - 1, j], xdev(e))
                if s < HALF and j in halves(i, s + 1):
                    send(ref, ref, ring_s.at[p, i, s, j], ring_r.at[p, i, s, j], xdev(e))
                send(ref, ref, cc_s.at[p, i, s - 1, j], cc_r.at[p, i, s - 1, j], partner)

    def cc_wait(p):
        arrived(gbuf.at[kp[p], w, 1 - c], co_s.at[p], co_r.at[p], partner)
        for s in range(1, HALF + 1):
            for i, e in enumerate((1, -1)):
                for j in halves(i, s):
                    ref = blk(p, e, s, j, 1 - c)
                    arrived(ref, cc_s.at[p, i, s - 1, j], cc_r.at[p, i, s - 1, j], partner)

    def z_send(above):
        ref = xbuf.at[:, :, zq, c, zh]
        for d in (4, 3, 5, 2, 6, 1, 7):

            @pl.when(z + d < NZ if above else z + d >= NZ)
            def _():
                pltpu.make_async_remote_copy(
                    src_ref=ref, dst_ref=ref, send_sem=zr_s.at[d], recv_sem=zr_r.at[d],
                    device_id=zdev(d), device_id_type=MESH,
                ).start()

    def z_wait():
        for d in range(1, NZ):
            zz = lax.rem(z + NZ - d, NZ)
            arrived(xbuf.at[:, :, zz // 2, c, lax.rem(zz, 2)], zr_s.at[d], zr_r.at[d], zdev(d))

    def z_sent():
        ref = xbuf.at[:, :, zq, c, zh]
        for d in range(1, NZ):
            pltpu.make_async_remote_copy(
                src_ref=ref, dst_ref=ref, send_sem=zr_s.at[d], recv_sem=zr_r.at[d],
                device_id=zdev(d), device_id_type=MESH,
            ).wait_send()

    def t3_dot(n):
        lhs = gbuf[k, :, c].reshape(256, 1536)
        out = lax.dot_general(
            lhs, wv[pl.ds(n * 512, 512), :], (((1,), (1,)), ((), ())), preferred_element_type=F32
        )
        part[:, :, :, pl.ds(n * 512, 512)] = out.astype(BF16).reshape(2, NZ, 16, 512)

    order = (4, 3, 5, 2, 6, 1, 7, 0)

    def t3_send():
        for d in order:
            zz = lax.rem(z + d, NZ)
            send(part.at[1 - yl, zz], rb1.at[d], t1_s.at[d], t1_r.at[d], yldev)

    def t3_pair(d):
        zz = lax.rem(z + d, NZ)
        arrived(rb1.at[d], t1_s.at[d], t1_r.at[d], yldev)
        both = part[yl, zz].astype(F32) + rb1[d].astype(F32)
        sb[d] = both.astype(BF16)

    def t3_out(d):
        if d:
            send(sb.at[d], rb2.at[d], t2_s.at[d], t2_r.at[d], zdev(d))

    def t3_final():
        total = sb[0].astype(F32)
        for d in range(1, NZ):
            arrived(rb2.at[d], t2_s.at[d], t2_r.at[d], zdev(d))
            total = total + rb2[d].astype(F32)
        gi_out[...] = total.astype(BF16)

    win = pl.ds(pl.multiple_of(c * 128, 128), 256)
    owin = pl.ds(pl.multiple_of((1 - c) * 128, 128), 256)

    def xc_send():
        ref = xbuf.at[:, :, :, c, :, :, owin]
        send(ref, ref, xc_s, xc_r, partner)

    def xc_wait():
        ref = xbuf.at[:, :, :, 1 - c, :, :, win]
        arrived(ref, xc_s, xc_r, partner)

    def t4(p):
        xt[...] = xbuf[kp[p], :, :, :, :, :, win].reshape(512, 256).T

        def step(n, _):
            col = pl.ds(pl.multiple_of(n * 512, 512), 512)
            rhs = gbuf[kp[p], :, :, :, :, col].reshape(512, 512)
            out = jnp.dot(xt[...], rhs, preferred_element_type=F32)
            if p == 0:
                acc[:, col] = out
            else:
                acc[:, col] += out
            return 0

        lax.fori_loop(0, 3, step, 0)

    ring_start(0)
    xa_send(1)
    xa_send(3)
    ye_send(1)
    ye_send(3)
    keep = pltpu.make_async_copy(g_own, gbuf.at[k, w, c], loc_sem.at[0])
    keep.start()
    xa_wait(1)
    xa_wait(3)
    xa_send(2)
    ye_send(2)
    ring_adv(0, 1)
    loads[0].wait()
    ring_adv(0, 2)
    xa_wait(2)
    ref = xbuf.at[:, yl, zq, c, zh]
    send(ref, ref, yl_s, yl_r, yldev)
    ring_adv(0, 3)
    arrived(xbuf.at[:, 1 - yl, zq, c, zh], yl_s, yl_r, yldev)
    z_send(False)
    ye_wait(3)
    ring_start(1)
    ye_wait(1)
    ring_start(2)
    loads[1].wait()
    keep.wait()
    ring_adv(0, 4)
    t3_dot(0)
    t3_dot(1)
    ring_adv(1, 1)
    t3_dot(2)
    ring_adv(2, 1)
    t3_send()
    ye_wait(2)
    ring_start(3)

    @pl.when(z < NZ - 1)
    def _():
        pl.semaphore_wait(in_sem, NZ - 1 - z)

    z_send(True)
    ring_adv(1, 2)
    late = None
    for n, d in enumerate(order):
        t3_pair(d)
        if late is not None:
            t3_out(late)
        late = d
        if n == 2:
            ring_adv(2, 2)
        if n == 4:
            ring_adv(3, 1)
        if n == 6:
            ring_adv(1, 3)
    ring_adv(2, 3)
    ring_adv(3, 2)
    ring_adv(1, 4)
    ring_adv(2, 4)
    ring_adv(3, 3)
    ring_adv(3, 4)
    z_wait()
    xc_send()
    xc_wait()
    for p in range(4):
        cc_wait(p)
        t4(p)
    gw_out[...] = acc[pl.ds(pl.multiple_of(c * 64, 64), 192), :]
    t3_final()
    z_sent()
    for cp in sends:
        cp.wait_send()


def body(saved_input, grad_out, weight, samples, correct, prompt_ids):
    dma = pltpu.SemaphoreType.DMA
    vm = pl.BlockSpec(memory_space=pltpu.VMEM)
    gw, gi = pl.pallas_call(
        kernel,
        out_shape=(
            pltpu.VMEM((192, 1536), F32),
            pltpu.VMEM((16, 1536), BF16),
        ),
        in_specs=[vm, vm, pl.BlockSpec(memory_space=pl.ANY), vm, vm, vm],
        out_specs=(vm, vm),
        scratch_shapes=[
            pltpu.VMEM((2, 16, 1536), BF16),
            pltpu.VMEM((NK, NX, 2, 2, 16, 1536), BF16),
            pltpu.VMEM((NK, 2, 4, 2, 2, 16, 384), BF16),
            pltpu.VMEM((1536, 1536), BF16),
            pltpu.VMEM((2, NZ, 16, 1536), BF16),
            pltpu.VMEM((NZ, 16, 1536), BF16),
            pltpu.VMEM((NZ, 16, 1536), BF16),
            pltpu.VMEM((NZ, 16, 1536), BF16),
            pltpu.VMEM((256, 1536), F32),
            pltpu.VMEM((256, 512), BF16),
            dma((3,)),
            dma((4, 2, HALF, 2)), dma((4, 2, HALF, 2)),
            dma((4,)), dma((4,)),
            dma((4, 2, HALF, 2)), dma((4, 2, HALF, 2)),
            dma((3,)), dma((3,)),
            dma((3,)), dma((3,)),
            dma, dma,
            dma((NZ,)), dma((NZ,)),
            dma, dma,
            dma((NZ,)), dma((NZ,)),
            dma((NZ,)), dma((NZ,)),
            pltpu.SemaphoreType.REGULAR,
        ],
        compiler_params=pltpu.CompilerParams(
            collective_id=0, has_side_effects=True, vmem_limit_bytes=56 * 1024 * 1024
        ),
        cost_estimate=pl.CostEstimate(flops=3_000_000_000, bytes_accessed=8_000_000, transcendentals=0),
    )(grad_out, saved_input, weight, samples[None, :], correct[None, :], prompt_ids[None, :])
    return gi, gw


def solution(mesh):
    in_specs = (
        P(("replica", "hidden"), "width"),
        P(("replica", "width"), "hidden"),
        P("width", "hidden"),
        P(),
        P(),
        P("replica"),
    )
    out_specs = (P(("replica", "hidden"), "width"), P(("width", "replica"), "hidden"))
    return jax.shard_map(body, mesh=mesh, in_specs=in_specs, out_specs=out_specs, check_vma=False)
```

time: 79.4 us -> 66.6 us (0.84)
  Pallas kernels: 71.4 us -> 64.2 us
  local copies, waits for them, and re-layouts: 4.54 us -> 1.64 us
  other arithmetic: 2.49 us -> 0 us
    pallas_call x1, Pallas kernels: 71.4 us -> 64.2 us  [body(): pl.pallas_call(kernel, out_shape=(pltpu.VMEM((192, 1536), F32), pltpu.VME...]
    unnamed x2, local copies, waits for them, and re-layouts: 3.78 us -> 1.64 us
    convert_element_type x2 -> x0, other arithmetic: 1.63 us -> none  [the longest x1 1.62 us: body(): (grad_out.astype(F32) * weights_own[:, None]).astype(BF16)]
where the time goes in v2:
time: 66.6 us; the launch traced here: 66.5 us
  Pallas kernels  64.2 us (96%)
  local copies, waits for them, and re-layouts  1.64 us (2%)
    pallas_call x1, Pallas kernels, body(): pl.pallas_call(kernel, out_shape=(pltpu.VMEM((192, 1536), F32), pltpu.VME...  64.2 us
    unnamed x2, local copies, waits for them, and re-layouts  1.64 us

profile of v2, /device:TPU:1, one launch (start us, length us, event | category | flops | bytes accessed | tf_op | source)
XLA Modules:
  0.0 66.5 jit_solution(14239101652274192241)
XLA Ops:
  0.6 64.2 %shard_map.77 = (f32[192,1536]{1,0:T(8,128)S(1)}, bf16[16,1536]{1,0:T(8,128)(2,1)S(1)}) custom-call(bf16[32,1536]{1,0:T(8,128)(2,1)} %g_in.1, bf16[16,1536]{1,0:T(8,128)(2,1)} %x_in.1, bf16[1536,1536]{1,0:T(8,128)(2,1)} %w_hbm.1, s32[1,64]{1,0:T(1,128)} %bitcast.4, s32[1,64]{1,0:T(1,128)} %bitcast.5, s32[1,256]{1,0:T(1,128)} %bitcast.3), custom_call_target="tpu_custom_call" | custom-call | flops 3000000000 | bytes 8000000 | tf_op jit(solution)/shard_map/pallas_call | solution.py:310
  64.8 0.6 copy.10
  65.4 1.0 %copy.11 = f32[192,1536]{1,0:T(8,128)} copy(f32[192,1536]{1,0:T(8,128)S(1)} %get-tuple-element.7) | data formatting | bytes 2359296

commit v3 on v2

--- a/solution.py
+++ b/solution.py
@@ -18,9 +18,9 @@
 
 def kernel(
     g_in, x_in, w_hbm, smp, cor, ids, gw_out, gi_out,
-    g_own, gbuf, xbuf, wv, part, rb1, sb, rb2, acc, xt,
-    loc_sem, ring_s, ring_r, co_s, co_r, cc_s, cc_r, ye_s, ye_r, xa_s, xa_r,
-    yl_s, yl_r, zr_s, zr_r, xc_s, xc_r, t1_s, t1_r, t2_s, t2_r, in_sem,
+    g_raw, g_own, gbuf, xbuf, wv, part, rb1, sb, rb2, acc, xt,
+    loc_sem, ring_s, ring_r, co_s, co_r, cc_s, cc_r, ye_s, ye_r, xa_s, xa_r, an_s, an_r,
+    zr_s, zr_r, xc_s, xc_r, t1_s, t1_r, t2_s, t2_r, in_sem, pin_sem,
 ):
     h = lax.axis_index("hidden")
     w = lax.axis_index("width")
@@ -58,8 +58,18 @@
     kp = [lax.rem(k + s, NK) for s in shift]
 
     bar = pltpu.get_barrier_semaphore()
-    for dev in (xdev(1), xdev(-1), kdev(1), kdev(3), yldev, partner):
+    y_peers = [(dk, dy) for dk in (1, 3, 2, 0) for dy in (0, 1) if dk or dy]
+
+    def ydev(dk, dy):
+        return {"hidden": (1 - yl if dy else yl) * NZ + z, **kdev(dk)}
+
+    for dev in (xdev(1), xdev(-1), *(ydev(*at) for at in y_peers)):
         pl.semaphore_signal(bar, inc=1, device_id=dev, device_id_type=MESH)
+
+    @pl.when(c == 1)
+    def _():
+        pl.semaphore_signal(bar, inc=1, device_id=partner, device_id_type=MESH)
+
     for d in range(1, NZ):
 
         @pl.when(z + d < NZ)
@@ -72,8 +82,40 @@
         ),
         pltpu.make_async_copy(w_hbm, wv, loc_sem.at[2]),
     ]
+    raw = pltpu.make_async_copy(g_in, g_raw, loc_sem.at[3])
+    raw.start()
     for cp in loads:
         cp.start()
+
+    pl.semaphore_wait(bar, 10 - c + z)
+
+    @pl.when(c == 0)
+    def _():
+        pl.semaphore_signal(pin_sem, inc=1, device_id=partner, device_id_type=MESH)
+
+    for d in range(1, NZ):
+
+        @pl.when(z + d >= NZ)
+        def _():
+            pl.semaphore_signal(in_sem, inc=1, device_id=zdev(d), device_id_type=MESH)
+
+    def xa_copy(n, dk, dy):
+        to = lax.rem(k + dk, NK)
+        return pltpu.make_async_remote_copy(
+            src_ref=x_in.at[:, pl.ds(pl.multiple_of(to * 384, 384), 384)],
+            dst_ref=xbuf.at[k, yl, zq, c, zh],
+            send_sem=xa_s.at[n], recv_sem=xa_r.at[n], device_id=ydev(dk, dy), device_id_type=MESH,
+        )
+
+    def xa_wait():
+        for n, (dk, dy) in enumerate(y_peers):
+            frm = lax.rem(k + NK - dk, NK)
+            arrived(xbuf.at[frm, 1 - yl if dy else yl, zq, c, zh], xa_s.at[n], xa_r.at[n], partner)
+
+    for n, at in enumerate(y_peers):
+        cp = xa_copy(n, *at)
+        cp.start()
+        sends.append(cp)
 
     total = smp[...].astype(F32)
     good = cor[...].astype(F32)
@@ -89,25 +131,8 @@
     mine = rows == lax.broadcasted_iota(jnp.int32, (32, 256), 1)
     weight = jnp.sum(jnp.where(mine, jnp.broadcast_to(picked, (32, 256)), 0.0), axis=1, keepdims=True)
     weight = weight.astype(BF16).astype(F32)
-    g_own[...] = (g_in[...].astype(F32) * weight).astype(BF16).reshape(2, 16, 1536)
-
-    pl.semaphore_wait(bar, 6 + z)
-    for d in range(1, NZ):
-
-        @pl.when(z + d >= NZ)
-        def _():
-            pl.semaphore_signal(in_sem, inc=1, device_id=zdev(d), device_id_type=MESH)
-
-    def xa_send(d):
-        to = lax.rem(k + d, NK)
-        send(
-            x_in.at[:, pl.ds(pl.multiple_of(to * 384, 384), 384)],
-            xbuf.at[k, yl, zq, c, zh], xa_s.at[d - 1], xa_r.at[d - 1], kdev(d),
-        )
-
-    def xa_wait(d):
-        frm = lax.rem(k + NK - d, NK)
-        arrived(xbuf.at[frm, yl, zq, c, zh], xa_s.at[d - 1], xa_r.at[d - 1], kdev(d))
+    raw.wait()
+    g_own[...] = (g_raw[...].astype(F32) * weight).astype(BF16).reshape(2, 16, 1536)
 
     def ye_send(d):
         send(g_own, gbuf.at[k, w, c], ye_s.at[d - 1], ye_r.at[d - 1], kdev(d))
@@ -116,39 +141,61 @@
         frm = lax.rem(k + NK - d, NK)
         arrived(gbuf.at[frm, w, c], ye_s.at[d - 1], ye_r.at[d - 1], kdev(d))
 
-    def blk(p, e, s, j, cc):
-        m = lax.rem(w - e * s + NX, NX)
-        return gbuf.at[kp[p], m, cc, j]
-
-    def halves(i, s):
-        return (0, 1) if s < HALF else (i,)
+    def away(e, s):
+        return lax.rem(w - e * s + NX, NX)
+
+    def pieces(p, e, s, cc):
+        ref = gbuf.at[kp[p], away(e, s), cc]
+        if p in (1, 2):
+            return [(0, ref)] if s < HALF else []
+        if s < HALF:
+            return [(0, ref.at[0]), (1, ref.at[1])]
+        j = 0 if e == 1 else 1
+        return [(j, ref.at[j])]
 
     def ring_start(p):
         own = gbuf.at[kp[p], w, c]
-        for j in (0, 1):
+        for j in (0,) if p in (1, 2) else (0, 1):
             for i, e in enumerate((1, -1)):
-                src = g_own.at[j] if p == 0 else own.at[j]
-                send(src, own.at[j], ring_s.at[p, i, 0, j], ring_r.at[p, i, 0, j], xdev(e))
-        send(g_own if p == 0 else own, own, co_s.at[p], co_r.at[p], partner)
+                dst = own if p in (1, 2) else own.at[j]
+                src = g_own.at[j] if p == 0 else dst
+                send(src, dst, ring_s.at[p, i, 0, j], ring_r.at[p, i, 0, j], xdev(e))
 
     def ring_adv(p, s):
-        for j in (0, 1):
+        for n in (0, 1):
             for i, e in enumerate((1, -1)):
-                if j not in halves(i, s):
+                here = pieces(p, e, s, c)
+                if n >= len(here):
                     continue
-                ref = blk(p, e, s, j, c)
+                j, ref = here[n]
                 arrived(ref, ring_s.at[p, i, s - 1, j], ring_r.at[p, i, s - 1, j], xdev(e))
-                if s < HALF and j in halves(i, s + 1):
+                if s < HALF and j in [q for q, _ in pieces(p, e, s + 1, c)]:
                     send(ref, ref, ring_s.at[p, i, s, j], ring_r.at[p, i, s, j], xdev(e))
-                send(ref, ref, cc_s.at[p, i, s - 1, j], cc_r.at[p, i, s - 1, j], partner)
+
+    def anti_send():
+        ref = gbuf.at[k, away(1, HALF), c]
+        for n, d in enumerate((1, 3)):
+            send(ref, ref, an_s.at[n], an_r.at[n], kdev(d))
+
+    def anti_wait(p):
+        n = 1 if p == 1 else 0
+        arrived(gbuf.at[kp[p], away(1, HALF), c], an_s.at[n], an_r.at[n], partner)
+
+    def cc_send(p):
+        ref = gbuf.at[kp[p], :, c]
+        send(ref, ref, co_s.at[p], co_r.at[p], partner)
+
+    def cc_last(n, e, s):
+        ref = gbuf.at[kp[3], away(e, s), c]
+        send(ref, ref, cc_s.at[n], cc_r.at[n], partner)
 
     def cc_wait(p):
-        arrived(gbuf.at[kp[p], w, 1 - c], co_s.at[p], co_r.at[p], partner)
-        for s in range(1, HALF + 1):
-            for i, e in enumerate((1, -1)):
-                for j in halves(i, s):
-                    ref = blk(p, e, s, j, 1 - c)
-                    arrived(ref, cc_s.at[p, i, s - 1, j], cc_r.at[p, i, s - 1, j], partner)
+        if p < 3:
+            arrived(gbuf.at[kp[p], :, 1 - c], co_s.at[p], co_r.at[p], partner)
+            return
+        for n in range(NX):
+            e, s = (1, n) if n <= HALF else (-1, n - HALF)
+            arrived(gbuf.at[kp[3], away(e, s), 1 - c], cc_s.at[n], cc_r.at[n], partner)
 
     def z_send(above):
         ref = xbuf.at[:, :, zq, c, zh]
@@ -225,79 +272,102 @@
             out = jnp.dot(xt[...], rhs, preferred_element_type=F32)
             if p == 0:
                 acc[:, col] = out
+            elif p < 3:
+                acc[:, col] += out
             else:
-                acc[:, col] += out
+
+                @pl.when(c == 0)
+                def _():
+                    gw_out[:, col] = acc[pl.ds(0, 192), col] + out[:192]
+
+                @pl.when(c == 1)
+                def _():
+                    gw_out[:, col] = acc[pl.ds(64, 192), col] + out[64:]
+
             return 0
 
         lax.fori_loop(0, 3, step, 0)
 
+    late = []
+
+    def t3_next(count):
+        for _ in range(count):
+            d = order[len(late)]
+            t3_pair(d)
+            if late:
+                t3_out(late[-1])
+            late.append(d)
+
     ring_start(0)
-    xa_send(1)
-    xa_send(3)
     ye_send(1)
     ye_send(3)
+    ye_send(2)
     keep = pltpu.make_async_copy(g_own, gbuf.at[k, w, c], loc_sem.at[0])
     keep.start()
-    xa_wait(1)
-    xa_wait(3)
-    xa_send(2)
-    ye_send(2)
     ring_adv(0, 1)
     loads[0].wait()
+    xa_wait()
+    z_send(False)
     ring_adv(0, 2)
-    xa_wait(2)
-    ref = xbuf.at[:, yl, zq, c, zh]
-    send(ref, ref, yl_s, yl_r, yldev)
-    ring_adv(0, 3)
-    arrived(xbuf.at[:, 1 - yl, zq, c, zh], yl_s, yl_r, yldev)
-    z_send(False)
     ye_wait(3)
     ring_start(1)
+    ring_adv(0, 3)
     ye_wait(1)
     ring_start(2)
+    keep.wait()
     loads[1].wait()
-    keep.wait()
     ring_adv(0, 4)
     t3_dot(0)
     t3_dot(1)
+    t3_dot(2)
     ring_adv(1, 1)
-    t3_dot(2)
-    ring_adv(2, 1)
     t3_send()
     ye_wait(2)
     ring_start(3)
+    ring_adv(2, 1)
 
     @pl.when(z < NZ - 1)
     def _():
         pl.semaphore_wait(in_sem, NZ - 1 - z)
 
     z_send(True)
+    t3_next(2)
     ring_adv(1, 2)
-    late = None
-    for n, d in enumerate(order):
-        t3_pair(d)
-        if late is not None:
-            t3_out(late)
-        late = d
-        if n == 2:
-            ring_adv(2, 2)
-        if n == 4:
-            ring_adv(3, 1)
-        if n == 6:
-            ring_adv(1, 3)
+    anti_send()
+    t3_next(2)
+    ring_adv(3, 1)
+    t3_next(2)
+    ring_adv(2, 2)
+    t3_next(2)
+    ring_adv(3, 2)
+
+    @pl.when(c == 1)
+    def _():
+        pl.semaphore_wait(pin_sem, 1)
+
+    cc_send(0)
+    cc_last(0, 1, 0)
+    cc_last(1, 1, 1)
+    cc_last(5, -1, 1)
+    cc_last(2, 1, 2)
+    cc_last(6, -1, 2)
+    ring_adv(1, 3)
+    anti_wait(1)
+    cc_send(1)
     ring_adv(2, 3)
-    ring_adv(3, 2)
-    ring_adv(1, 4)
-    ring_adv(2, 4)
+    anti_wait(2)
+    cc_send(2)
     ring_adv(3, 3)
-    ring_adv(3, 4)
+    cc_last(3, 1, 3)
+    cc_last(7, -1, 3)
     z_wait()
     xc_send()
+    ring_adv(3, 4)
+    cc_last(4, 1, 4)
     xc_wait()
     for p in range(4):
         cc_wait(p)
         t4(p)
-    gw_out[...] = acc[pl.ds(pl.multiple_of(c * 64, 64), 192), :]
     t3_final()
     z_sent()
     for cp in sends:
@@ -307,15 +377,17 @@
 def body(saved_input, grad_out, weight, samples, correct, prompt_ids):
     dma = pltpu.SemaphoreType.DMA
     vm = pl.BlockSpec(memory_space=pltpu.VMEM)
+    hbm = pl.BlockSpec(memory_space=pl.ANY)
     gw, gi = pl.pallas_call(
         kernel,
         out_shape=(
             pltpu.VMEM((192, 1536), F32),
             pltpu.VMEM((16, 1536), BF16),
         ),
-        in_specs=[vm, vm, pl.BlockSpec(memory_space=pl.ANY), vm, vm, vm],
+        in_specs=[hbm, hbm, hbm, vm, vm, vm],
         out_specs=(vm, vm),
         scratch_shapes=[
+            pltpu.VMEM((32, 1536), BF16),
             pltpu.VMEM((2, 16, 1536), BF16),
             pltpu.VMEM((NK, NX, 2, 2, 16, 1536), BF16),
             pltpu.VMEM((NK, 2, 4, 2, 2, 16, 384), BF16),
@@ -326,17 +398,18 @@
             pltpu.VMEM((NZ, 16, 1536), BF16),
             pltpu.VMEM((256, 1536), F32),
             pltpu.VMEM((256, 512), BF16),
-            dma((3,)),
-            dma((4, 2, HALF, 2)), dma((4, 2, HALF, 2)),
-            dma((4,)), dma((4,)),
+            dma((4,)),
             dma((4, 2, HALF, 2)), dma((4, 2, HALF, 2)),
             dma((3,)), dma((3,)),
+            dma((NX,)), dma((NX,)),
             dma((3,)), dma((3,)),
-            dma, dma,
+            dma((7,)), dma((7,)),
+            dma((2,)), dma((2,)),
             dma((NZ,)), dma((NZ,)),
             dma, dma,
             dma((NZ,)), dma((NZ,)),
             dma((NZ,)), dma((NZ,)),
+            pltpu.SemaphoreType.REGULAR,
             pltpu.SemaphoreType.REGULAR,
         ],
         compiler_params=pltpu.CompilerParams(

time: 66.6 us -> 60.6 us (0.910)
  the two profiles are of different devices: /device:TPU:1 before, /device:TPU:4 now
where the time goes in v3:
time: 60.6 us; the launch traced here: 60.4 us
  Pallas kernels  58.1 us (96%)
  local copies, waits for them, and re-layouts  1.64 us (3%)
  between operations  0.64 us (1%)
    pallas_call x1, Pallas kernels, body(): pl.pallas_call(kernel, out_shape=(pltpu.VMEM((192, 1536), F32), pltpu.VME...  58.1 us
    unnamed x2, local copies, waits for them, and re-layouts  1.64 us

profile of v3, /device:TPU:4, one launch (start us, length us, event | category | flops | bytes accessed | tf_op | source)
XLA Modules:
  0.0 60.4 jit_solution(4706594661789038908)
XLA Ops:
  0.6 58.1 %shard_map.77 = (f32[192,1536]{1,0:T(8,128)S(1)}, bf16[16,1536]{1,0:T(8,128)(2,1)S(1)}) custom-call(bf16[32,1536]{1,0:T(8,128)(2,1)} %g_in.1, bf16[16,1536]{1,0:T(8,128)(2,1)} %x_in.1, bf16[1536,1536]{1,0:T(8,128)(2,1)} %w_hbm.1, s32[1,64]{1,0:T(1,128)} %bitcast.4, s32[1,64]{1,0:T(1,128)} %bitcast.5, s32[1,256]{1,0:T(1,128)} %bitcast.3), custom_call_target="tpu_custom_call" | custom-call | flops 3000000000 | bytes 8000000 | tf_op jit(solution)/shard_map/pallas_call | solution.py:381
  58.8 0.6 %copy.10 = bf16[16,1536]{1,0:T(8,128)(2,1)} copy(bf16[16,1536]{1,0:T(8,128)(2,1)S(1)} %get-tuple-element.6) | data formatting | bytes 98304
  59.4 1.0 %copy.11 = f32[192,1536]{1,0:T(8,128)} copy(f32[192,1536]{1,0:T(8,128)S(1)} %get-tuple-element.7) | data formatting | bytes 2359296

commit v4 on v3

--- a/solution.py
+++ b/solution.py
@@ -18,7 +18,7 @@
 
 def kernel(
     g_in, x_in, w_hbm, smp, cor, ids, gw_out, gi_out,
-    g_raw, g_own, gbuf, xbuf, wv, part, rb1, sb, rb2, acc, xt,
+    v_smp, v_cor, v_ids, g_raw, g_own, gbuf, xbuf, wv, part, rb1, sb, rb2, acc, xt,
     loc_sem, ring_s, ring_r, co_s, co_r, cc_s, cc_r, ye_s, ye_r, xa_s, xa_r, an_s, an_r,
     zr_s, zr_r, xc_s, xc_r, t1_s, t1_r, t2_s, t2_r, in_sem, pin_sem,
 ):
@@ -82,10 +82,33 @@
         ),
         pltpu.make_async_copy(w_hbm, wv, loc_sem.at[2]),
     ]
-    raw = pltpu.make_async_copy(g_in, g_raw, loc_sem.at[3])
-    raw.start()
+    raw = [
+        pltpu.make_async_copy(src, dst, loc_sem.at[3 + n])
+        for n, (src, dst) in enumerate(((smp, v_smp), (cor, v_cor), (ids, v_ids), (g_in, g_raw)))
+    ]
+    for cp in raw:
+        cp.start()
     for cp in loads:
         cp.start()
+
+    for cp in raw[:3]:
+        cp.wait()
+    total = v_smp[...].astype(F32)
+    good = v_cor[...].astype(F32)
+    missing = jnp.ones_like(total)
+    for j in range(K):
+        missing = missing * jnp.maximum(total - good - j, 0.0) / (total - j)
+    pass_at_k = 1.0 - missing
+    prompts = lax.broadcasted_iota(jnp.int32, (64, 64), 0) == lax.broadcasted_iota(jnp.int32, (64, 64), 1)
+    column = jnp.sum(jnp.where(prompts, jnp.broadcast_to(pass_at_k, (64, 64)), 0.0), axis=1, keepdims=True)
+    match = lax.broadcasted_iota(jnp.int32, (64, 256), 0) == jnp.broadcast_to(v_ids[...], (64, 256))
+    picked = jnp.sum(jnp.where(match, jnp.broadcast_to(column, (64, 256)), 0.0), axis=0, keepdims=True)
+    rows = lax.broadcasted_iota(jnp.int32, (32, 256), 0) + w * 32
+    mine = rows == lax.broadcasted_iota(jnp.int32, (32, 256), 1)
+    weight = jnp.sum(jnp.where(mine, jnp.broadcast_to(picked, (32, 256)), 0.0), axis=1, keepdims=True)
+    weight = weight.astype(BF16).astype(F32)
+    raw[3].wait()
+    g_own[...] = (g_raw[...].astype(F32) * weight).astype(BF16).reshape(2, 16, 1536)
 
     pl.semaphore_wait(bar, 10 - c + z)
 
@@ -111,28 +134,6 @@
         for n, (dk, dy) in enumerate(y_peers):
             frm = lax.rem(k + NK - dk, NK)
             arrived(xbuf.at[frm, 1 - yl if dy else yl, zq, c, zh], xa_s.at[n], xa_r.at[n], partner)
-
-    for n, at in enumerate(y_peers):
-        cp = xa_copy(n, *at)
-        cp.start()
-        sends.append(cp)
-
-    total = smp[...].astype(F32)
-    good = cor[...].astype(F32)
-    missing = jnp.ones_like(total)
-    for j in range(K):
-        missing = missing * jnp.maximum(total - good - j, 0.0) / (total - j)
-    pass_at_k = 1.0 - missing
-    prompts = lax.broadcasted_iota(jnp.int32, (64, 64), 0) == lax.broadcasted_iota(jnp.int32, (64, 64), 1)
-    column = jnp.sum(jnp.where(prompts, jnp.broadcast_to(pass_at_k, (64, 64)), 0.0), axis=1, keepdims=True)
-    match = lax.broadcasted_iota(jnp.int32, (64, 256), 0) == jnp.broadcast_to(ids[...], (64, 256))
-    picked = jnp.sum(jnp.where(match, jnp.broadcast_to(column, (64, 256)), 0.0), axis=0, keepdims=True)
-    rows = lax.broadcasted_iota(jnp.int32, (32, 256), 0) + w * 32
-    mine = rows == lax.broadcasted_iota(jnp.int32, (32, 256), 1)
-    weight = jnp.sum(jnp.where(mine, jnp.broadcast_to(picked, (32, 256)), 0.0), axis=1, keepdims=True)
-    weight = weight.astype(BF16).astype(F32)
-    raw.wait()
-    g_own[...] = (g_raw[...].astype(F32) * weight).astype(BF16).reshape(2, 16, 1536)
 
     def ye_send(d):
         send(g_own, gbuf.at[k, w, c], ye_s.at[d - 1], ye_r.at[d - 1], kdev(d))
@@ -199,7 +200,7 @@
 
     def z_send(above):
         ref = xbuf.at[:, :, zq, c, zh]
-        for d in (4, 3, 5, 2, 6, 1, 7):
+        for d in (1, 2, 7, 3, 6, 4, 5):
 
             @pl.when(z + d < NZ if above else z + d >= NZ)
             def _():
@@ -228,7 +229,7 @@
         )
         part[:, :, :, pl.ds(n * 512, 512)] = out.astype(BF16).reshape(2, NZ, 16, 512)
 
-    order = (4, 3, 5, 2, 6, 1, 7, 0)
+    order = (1, 2, 7, 3, 6, 4, 5, 0)
 
     def t3_send():
         for d in order:
@@ -299,6 +300,10 @@
             late.append(d)
 
     ring_start(0)
+    for n, at in enumerate(y_peers):
+        cp = xa_copy(n, *at)
+        cp.start()
+        sends.append(cp)
     ye_send(1)
     ye_send(3)
     ye_send(2)
@@ -309,21 +314,22 @@
     xa_wait()
     z_send(False)
     ring_adv(0, 2)
+    ring_adv(0, 3)
     ye_wait(3)
     ring_start(1)
-    ring_adv(0, 3)
     ye_wait(1)
     ring_start(2)
+    ring_adv(0, 4)
+    ye_wait(2)
+    ring_start(3)
     keep.wait()
     loads[1].wait()
-    ring_adv(0, 4)
     t3_dot(0)
     t3_dot(1)
     t3_dot(2)
+    t3_send()
+    anti_send()
     ring_adv(1, 1)
-    t3_send()
-    ye_wait(2)
-    ring_start(3)
     ring_adv(2, 1)
 
     @pl.when(z < NZ - 1)
@@ -333,8 +339,7 @@
     z_send(True)
     t3_next(2)
     ring_adv(1, 2)
-    anti_send()
-    t3_next(2)
+    t3_next(1)
     ring_adv(3, 1)
     t3_next(2)
     ring_adv(2, 2)
@@ -351,23 +356,29 @@
     cc_last(5, -1, 1)
     cc_last(2, 1, 2)
     cc_last(6, -1, 2)
+    t3_next(1)
     ring_adv(1, 3)
     anti_wait(1)
     cc_send(1)
     ring_adv(2, 3)
+    ring_adv(3, 3)
+    z_wait()
+    xc_send()
     anti_wait(2)
     cc_send(2)
-    ring_adv(3, 3)
     cc_last(3, 1, 3)
     cc_last(7, -1, 3)
-    z_wait()
-    xc_send()
+    xc_wait()
+    cc_wait(0)
+    t4(0)
+    cc_wait(1)
+    t4(1)
     ring_adv(3, 4)
     cc_last(4, 1, 4)
-    xc_wait()
-    for p in range(4):
-        cc_wait(p)
-        t4(p)
+    cc_wait(2)
+    t4(2)
+    cc_wait(3)
+    t4(3)
     t3_final()
     z_sent()
     for cp in sends:
@@ -384,9 +395,12 @@
             pltpu.VMEM((192, 1536), F32),
             pltpu.VMEM((16, 1536), BF16),
         ),
-        in_specs=[hbm, hbm, hbm, vm, vm, vm],
+        in_specs=[hbm] * 6,
         out_specs=(vm, vm),
         scratch_shapes=[
+            pltpu.VMEM((1, 64), jnp.int32),
+            pltpu.VMEM((1, 64), jnp.int32),
+            pltpu.VMEM((1, 256), jnp.int32),
             pltpu.VMEM((32, 1536), BF16),
             pltpu.VMEM((2, 16, 1536), BF16),
             pltpu.VMEM((NK, NX, 2, 2, 16, 1536), BF16),
@@ -398,7 +412,7 @@
             pltpu.VMEM((NZ, 16, 1536), BF16),
             pltpu.VMEM((256, 1536), F32),
             pltpu.VMEM((256, 512), BF16),
-            dma((4,)),
+            dma((7,)),
             dma((4, 2, HALF, 2)), dma((4, 2, HALF, 2)),
             dma((3,)), dma((3,)),
             dma((NX,)), dma((NX,)),

time: 60.6 us -> 63.8 us (1.053)
  the two profiles are of different devices: /device:TPU:4 before, /device:TPU:2 now
where the time goes in v4:
time: 63.8 us; the launch traced here: 63.7 us
  Pallas kernels  61.4 us (96%)
  local copies, waits for them, and re-layouts  1.64 us (3%)
  between operations  0.64 us (1%)
    pallas_call x1, Pallas kernels, body(): pl.pallas_call(kernel, out_shape=(pltpu.VMEM((192, 1536), F32), pltpu.VME...  61.4 us
    unnamed x2, local copies, waits for them, and re-layouts  1.64 us

profile of v4, /device:TPU:2, one launch (start us, length us, event | category | flops | bytes accessed | tf_op | source)
XLA Modules:
  0.0 63.7 jit_solution(11009954266553361086)
XLA Ops:
  0.6 61.4 %shard_map.77 = (f32[192,1536]{1,0:T(8,128)S(1)}, bf16[16,1536]{1,0:T(8,128)(2,1)S(1)}) custom-call(bf16[32,1536]{1,0:T(8,128)(2,1)} %g_in.1, bf16[16,1536]{1,0:T(8,128)(2,1)} %x_in.1, bf16[1536,1536]{1,0:T(8,128)(2,1)} %w_hbm.1, s32[1,64]{1,0:T(1,128)} %bitcast.4, s32[1,64]{1,0:T(1,128)} %bitcast.5, s32[1,256]{1,0:T(1,128)} %bitcast.3), custom_call_target="tpu_custom_call" | custom-call | flops 3000000000 | bytes 8000000 | tf_op jit(solution)/shard_map/pallas_call | solution.py:392
  62.1 0.6 copy.10
  62.7 1.0 %copy.11 = f32[192,1536]{1,0:T(8,128)} copy(f32[192,1536]{1,0:T(8,128)S(1)} %get-tuple-element.7) | data formatting | bytes 2359296

commit v5 on v4

--- a/solution.py
+++ b/solution.py
@@ -200,7 +200,7 @@
 
     def z_send(above):
         ref = xbuf.at[:, :, zq, c, zh]
-        for d in (1, 2, 7, 3, 6, 4, 5):
+        for d in (4, 3, 5, 2, 6, 1, 7):
 
             @pl.when(z + d < NZ if above else z + d >= NZ)
             def _():
@@ -229,7 +229,7 @@
         )
         part[:, :, :, pl.ds(n * 512, 512)] = out.astype(BF16).reshape(2, NZ, 16, 512)
 
-    order = (1, 2, 7, 3, 6, 4, 5, 0)
+    order = (4, 3, 5, 2, 6, 1, 7, 0)
 
     def t3_send():
         for d in order:
@@ -310,13 +310,13 @@
     keep = pltpu.make_async_copy(g_own, gbuf.at[k, w, c], loc_sem.at[0])
     keep.start()
     ring_adv(0, 1)
+    ring_adv(0, 2)
+    ye_wait(3)
+    ring_start(1)
     loads[0].wait()
     xa_wait()
     z_send(False)
-    ring_adv(0, 2)
     ring_adv(0, 3)
-    ye_wait(3)
-    ring_start(1)
     ye_wait(1)
     ring_start(2)
     ring_adv(0, 4)
@@ -326,10 +326,10 @@
     loads[1].wait()
     t3_dot(0)
     t3_dot(1)
+    ring_adv(1, 1)
     t3_dot(2)
     t3_send()
     anti_send()
-    ring_adv(1, 1)
     ring_adv(2, 1)
 
     @pl.when(z < NZ - 1)
@@ -337,7 +337,6 @@
         pl.semaphore_wait(in_sem, NZ - 1 - z)
 
     z_send(True)
-    t3_next(2)
     ring_adv(1, 2)
     t3_next(1)
     ring_adv(3, 1)
@@ -356,7 +355,7 @@
     cc_last(5, -1, 1)
     cc_last(2, 1, 2)
     cc_last(6, -1, 2)
-    t3_next(1)
+    t3_next(3)
     ring_adv(1, 3)
     anti_wait(1)
     cc_send(1)

time: 63.8 us -> 61.9 us (0.970)
  the two profiles are of different devices: /device:TPU:2 before, /device:TPU:4 now
where the time goes in v5:
time: 61.9 us; the launch traced here: 61.7 us
  Pallas kernels  59.5 us (96%)
  local copies, waits for them, and re-layouts  1.64 us (3%)
  between operations  0.64 us (1%)
    pallas_call x1, Pallas kernels, body(): pl.pallas_call(kernel, out_shape=(pltpu.VMEM((192, 1536), F32), pltpu.VME...  59.5 us
    unnamed x2, local copies, waits for them, and re-layouts  1.64 us

profile of v5, /device:TPU:4, one launch (start us, length us, event | category | flops | bytes accessed | tf_op | source)
XLA Modules:
  0.0 61.7 jit_solution(15320453959846724441)
XLA Ops:
  0.6 59.5 %shard_map.77 = (f32[192,1536]{1,0:T(8,128)S(1)}, bf16[16,1536]{1,0:T(8,128)(2,1)S(1)}) custom-call(bf16[32,1536]{1,0:T(8,128)(2,1)} %g_in.1, bf16[16,1536]{1,0:T(8,128)(2,1)} %x_in.1, bf16[1536,1536]{1,0:T(8,128)(2,1)} %w_hbm.1, s32[1,64]{1,0:T(1,128)} %bitcast.4, s32[1,64]{1,0:T(1,128)} %bitcast.5, s32[1,256]{1,0:T(1,128)} %bitcast.3), custom_call_target="tpu_custom_call" | custom-call | flops 3000000000 | bytes 8000000 | tf_op jit(solution)/shard_map/pallas_call | solution.py:391
  60.1 0.6 %copy.10 = bf16[16,1536]{1,0:T(8,128)(2,1)} copy(bf16[16,1536]{1,0:T(8,128)(2,1)S(1)} %get-tuple-element.6) | data formatting | bytes 98304
  60.7 1.0 %copy.11 = f32[192,1536]{1,0:T(8,128)} copy(f32[192,1536]{1,0:T(8,128)S(1)} %get-tuple-element.7) | data formatting | bytes 2359296
